TPU v7x, 512 devices: a whole 4x8x8 slice. The times are simulated.
512 devices in a mesh: stream: 8 (over y), span: 16 (over z, core), vert: 4 (over x).
Axes of the slice: x: 4, y: 8, z: 8, core: 2. Of those that a mesh axis runs over, the one named last changes fastest.
Arguments:
- fields: float32 [5, 128, 256, 1024], P(None, 'vert', 'span', 'stream'), may hold values from -6 to 6
- solid_frac: float32 [128, 256, 1024], P('vert', 'span', 'stream'), may hold values from 0 to 1
- panels: float32 [32768, 5, 256], P(('stream', 'span', 'vert')), may hold values from -0.015625 to 0.015625
- panel_owner: int32 [32768, 1], P(('stream', 'span', 'vert')), may hold values from 0 to 63; in each aligned block of 64 rows (0 to 63, 64 to 127, ...) at most 2 rows name the same one
- deck_cells: int32 [4, 16, 8, 2048], P('vert', 'span', 'stream'), may hold values from 0 to 65535
- deck_geom: float32 [4, 16, 8, 3, 2048], P('vert', None, 'stream'), may hold values from -6 to 6
- strip_ids: int32 [4, 16, 8, 2048], P('vert', None, 'stream'), may hold values from 0 to 63, as said below
- mode_shapes: float32 [3, 64, 32], replicated, may hold values from -0.0034179688 to 0.0034179688
Outputs:
- new_fields: float32 [5, 128, 256, 1024], P(None, 'vert', 'span', 'stream')
- modal_force: float32 [32], replicated
Inputs may be any that keep to these rules, and one draw needn't show every extreme that they name: `panel_owner`: tile number s * 4 + v for along-deck tile s and vertical tile v. Among the 64 panels of one device no tile is named more than 2 times; some device names some tile exactly 2 times. `strip_ids`: cells of along-deck tile s belong to strips s * 4 to (s + 1) * 4 - 1.
All inputs are finite; a program needn't handle non-finite values.
Results may differ from a plain program's by a relative error of at most 0.00012.
Values sent between devices are 32-bit elements; how exact they have to be, the bound alone decides.
No kernel may reach another device: no remote copies, remote signals or barrier semaphores. Data moves between devices by JAX's collectives and lax.ppermute only.
A program may use at most 128 MiB of HBM per device.

v0:
```python
import math
import jax
import jax.numpy as jnp
from jax import lax
from jax.sharding import PartitionSpec as P

CAP = 2
time_step = 0.15
viscous = 0.05
heat_diff = 0.03
sound_sq = 1.0
buoyant = 0.5
penalty = 0.5
relax_time = 0.5
relax_depth = 8.0
wave_cols = 16


def extended(block, sides, width):
    for axis, dim in sides:
        count = lax.axis_size(axis)
        forward = [(i, i + 1) for i in range(count - 1)]
        backward = [(target, source) for source, target in forward]
        low = lax.ppermute(
            lax.slice_in_dim(block, block.shape[dim] - width, None, axis=dim), axis, forward
        )
        high = lax.ppermute(lax.slice_in_dim(block, 0, width, axis=dim), axis, backward)
        block = jnp.concatenate([low, block, high], axis=dim)
    return block


def wave_basis(heights, widths, total_z, total_y, spec):
    modes = jnp.arange(spec, dtype=jnp.int32)
    across = (modes % wave_cols)[:, None, None]
    upward = (modes // wave_cols)[:, None, None]
    period = total_y * total_z
    phase = (
        across * widths[None, None, :] * total_z + upward * heights[None, :, None] * total_y
    ) % period
    angle = phase.astype(jnp.float32) * (2.0 * math.pi / period)
    return jnp.concatenate([jnp.cos(angle), jnp.sin(angle)], axis=0)


def relax_weights(positions, limit):
    spots = positions.astype(jnp.float32)
    return jnp.where(positions < limit, jnp.exp(-spots / relax_depth) / relax_time, 0.0)


def rates(padded, solid_frac, relax_rate, target_plane):
    centre = padded[:, 1:-1, 1:-1, 1:-1]
    east_side = padded[:, 1:-1, 1:-1, 2:]
    west_side = padded[:, 1:-1, 1:-1, :-2]
    north_side = padded[:, 1:-1, 2:, 1:-1]
    south_side = padded[:, 1:-1, :-2, 1:-1]
    upper_side = padded[:, 2:, 1:-1, 1:-1]
    lower_side = padded[:, :-2, 1:-1, 1:-1]
    grad_x = 0.5 * (east_side - west_side)
    grad_y = 0.5 * (north_side - south_side)
    grad_z = 0.5 * (upper_side - lower_side)
    laplace = (
        east_side + west_side + north_side + south_side + upper_side + lower_side - 6.0 * centre
    )
    speed_x = centre[0]
    speed_y = centre[1]
    speed_z = centre[2]
    carried = speed_x * grad_x + speed_y * grad_y + speed_z * grad_z
    coeffs = jnp.array([viscous, viscous, viscous, viscous, heat_diff], jnp.float32)[
        :, None, None, None
    ]
    damping = solid_frac / penalty
    nudging = relax_rate[None, None, None, :] * (target_plane[:, :, :, None] - centre)
    common = coeffs * laplace - carried + nudging
    extra_terms = jnp.stack(
        [
            -grad_x[3] - damping * speed_x,
            -grad_y[3] - damping * speed_y,
            -grad_z[3] - damping * speed_z + buoyant * centre[4],
            -sound_sq * (grad_x[0] + grad_y[1] + grad_z[2]),
            jnp.zeros_like(speed_x),
        ]
    )
    return common + extra_terms


def pack_slots(flat_panels, target_tile, chosen, tile_count):
    running = jnp.cumsum(chosen, axis=0) - 1
    slot_rank = jnp.sum(chosen * running, axis=1)
    slot_index = target_tile * CAP + slot_rank
    dispatch = (
        slot_index[None, :] == jnp.arange(tile_count * CAP, dtype=jnp.int32)[:, None]
    ).astype(jnp.float32)
    return jnp.dot(dispatch, flat_panels, precision=lax.Precision.HIGHEST)


def strip_forces(traction, labels, strip_count):
    columns = jnp.arange(strip_count, dtype=jnp.int32)

    def add_row(running, item_pair):
        row_values, row_labels = item_pair
        member = (row_labels[:, None] == columns[None, :]).astype(jnp.float32)
        return (running + jnp.dot(row_values, member, precision=lax.Precision.HIGHEST), None)

    start_value = jnp.zeros((traction.shape[1], strip_count), jnp.float32)
    summed, ignored = lax.scan(add_row, start_value, (traction, labels))
    return summed


def on_device(
    fields, solid_frac, panels, panel_owner, deck_cells, deck_geom, strip_ids, mode_shapes
):
    depth_cells = fields.shape[1]
    span_cells = fields.shape[2]
    wind_cells = fields.shape[3]
    n_span = lax.axis_size("span")
    n_vert = lax.axis_size("vert")
    stream_pos = lax.axis_index("stream")
    span_pos = lax.axis_index("span")
    vert_pos = lax.axis_index("vert")
    tile_count = n_span * n_vert
    held_panels = panels.shape[0]
    spec_cols = panels.shape[2]
    flat_panels = panels.reshape(held_panels, 5 * spec_cols)
    target_tile = panel_owner[:, 0]
    chosen = (target_tile[:, None] == jnp.arange(tile_count, dtype=jnp.int32)[None, :]).astype(
        jnp.int32
    )
    outgoing = pack_slots(flat_panels, target_tile, chosen, tile_count)
    arrived = lax.all_to_all(
        outgoing.reshape(tile_count, CAP * 5 * spec_cols),
        ("span", "vert"),
        split_axis=0,
        concat_axis=0,
        tiled=True,
    )
    coeffs = jnp.sum(arrived.reshape(-1, 5 * spec_cols), axis=0)
    coeffs = coeffs.reshape(5, spec_cols)
    heights = vert_pos * depth_cells + jnp.arange(depth_cells, dtype=jnp.int32)
    widths = span_pos * span_cells + jnp.arange(span_cells, dtype=jnp.int32)
    wave_table = wave_basis(
        heights, widths, depth_cells * n_vert, span_cells * n_span, spec_cols // 2
    )
    wave_table = wave_table.reshape(spec_cols, depth_cells * span_cells)
    partial_value = jnp.dot(coeffs, wave_table, precision=lax.Precision.HIGHEST)
    inflow_plane = lax.psum(partial_value, "stream").reshape(5, depth_cells, span_cells)
    target_plane = inflow_plane + jnp.array([1.0, 0.0, 0.0, 0.0, 0.0], jnp.float32)[:, None, None]
    wind_first = stream_pos * wind_cells
    relax_rate = relax_weights(
        wind_first + jnp.arange(wind_cells, dtype=jnp.int32), wind_cells // 2
    )

    def advance(state):
        padded = extended(state, (("stream", 3), ("span", 2), ("vert", 1)), 1)
        return rates(padded, solid_frac, relax_rate, target_plane)

    first_update = fields + time_step * advance(fields)
    second_rate = advance(first_update)
    new_fields = 0.5 * (fields + first_update + time_step * second_rate)
    pressure = new_fields[3].reshape(-1)
    sampled = pressure[deck_cells[0, 0, 0]]
    strip_count = mode_shapes.shape[1]
    rows_all = lax.all_gather(sampled.reshape(1, 1, 1, -1), "span", axis=1, tiled=True)
    traction = rows_all[0, :, 0][:, None, :] * deck_geom[0, :, 0]
    forces = strip_forces(traction, strip_ids[0, :, 0], strip_count)
    modal_part = jnp.einsum("cj,cjm->m", forces, mode_shapes, precision=lax.Precision.HIGHEST)
    modal_force = lax.psum(modal_part, ("stream", "vert"))
    return (new_fields, modal_force)


def solution(mesh):
    return jax.shard_map(
        on_device,
        mesh=mesh,
        in_specs=(
            P(None, "vert", "span", "stream"),
            P("vert", "span", "stream"),
            P(("stream", "span", "vert"), None, None),
            P(("stream", "span", "vert"), None),
            P("vert", "span", "stream", None),
            P("vert", None, "stream", None, None),
            P("vert", None, "stream", None),
            P(),
        ),
        out_specs=(P(None, "vert", "span", "stream"), P()),
        check_vma=False,
    )
```

profile of v0, /device:TPU:64, one launch (start us, length us, event | category | flops | bytes accessed | tf_op | source)
XLA Modules:
  0.0 263.3 jit_solution(5278629360200519969)
XLA Ops:
  0.6 2.2 fusion.52
  5.3 4.5 %collective-permute-start.1 = (f32[5,32,16,1]{1,2,3,0:T(8,128)S(1)}, f32[5,32,16,1]{1,2,3,0:T(8,128)S(1)}, u32[]{:S(2)}, u32[]{:S(2)}) collective-permute-start(f32[5,32,16,1]{1,2,3,0:T(8,128)S(1)} %copy.56), channel_id=1, source_target_pairs={{0,64},{64,128},{128,192},{192,256},{256,320},{320,384},{384,448},... | collective-permute-start | bytes 30728 | tf_op jit(solution)/shard_map/ppermute | solution.py:24
  12.2 13.3 %all-to-all-start = ((f32[64,1,2560]{2,1,0:T(1,128)}), f32[64,1,2560]{2,1,0:T(1,128)}, u32[]{:S(2)}, u32[]{:S(2)}) async-start(f32[64,1,2560]{2,1,0:T(1,128)} %all_to_all.8), calls=%async_computation | async-start | bytes 1310720 | tf_op jit(solution)/shard_map/all_to_all | solution.py:128
  30.7 2.5 pad_maximum_fusion.39
  33.2 2.0 collective-permute-start.2
  35.2 2.3 collective-permute-start.3
  37.5 4.0 %collective-permute-done.2 = f32[5,32,1,130]{3,2,1,0:T(1,128)S(1)} collective-permute-done((f32[5,32,1,130]{3,2,1,0:T(1,128)S(1)}, f32[5,32,1,130]{3,2,1,0:T(1,128)S(1)}, u32[]{:S(2)}, u32[]{:S(2)}) %collective-permute-start.2) | collective-permute-done | bytes 83232 | tf_op jit(solution)/shard_map/ppermute | solution.py:27
  44.5 4.7 %collective-permute-start.5 = (f32[5,1,18,130]{3,2,1,0:T(8,128)S(1)}, f32[5,1,18,130]{3,2,1,0:T(8,128)S(1)}, u32[]{:S(2)}, u32[]{:S(2)}) collective-permute-start(f32[5,1,18,130]{3,2,1,0:T(8,128)S(1)} %get-tuple-element.71), channel_id=1, source_target_pairs={{0,1},{1,2},{2,3},{4,5},{5,6},{6,7},{8,9},{9,10},{10,11},{12,13},{... | collective-permute-start | bytes 140408 | tf_op jit(solution)/shard_map/ppermute | solution.py:24
  51.7 3.2 %broadcast_multiply_fusion.3 = (f32[5,32,16,128]{3,2,1,0:T(8,128)S(1)}, f32[5,32,16,128]{3,2,1,0:T(8,128)S(1)}) fusion(f32[5,1,18,130]{3,2,1,0:T(8,128)S(1)} %collective-permute-done.4, f32[5,32,1,130]{3,2,1,0:T(1,128)S(1)} %collective-permute-done.2, f32[5,32,16,1]{3,2,1,0:T(8,128)S(1)} %copy.37, f32[5,32,16,128]{3,2,1,0:T(8,128)S(1)} %copy-done.1, ...), kind=kLoop, calls=%fused_computation.50 | loop fusion | flops 5242880 | bytes 4212640 | tf_op jit(solution)/shard_map/mul | solution.py:59
  58.7 2.6 %reduce = f32[64,2560]{1,0:T(8,128)S(1)} reduce(f32[64,1,2560]{2,1,0:T(1,128)} %all-to-all-done, f32[]{:T(128)} %constant.123), dimensions={1}, to_apply=%all_to_all.7.reduce_sub_computation | reduce | bytes 1310724 | tf_op jit(solution)/shard_map/all_to_all | solution.py:128
  63.1 30.8 %psum.14 = f32[5,32,16]{2,1,0:T(8,128)S(1)} all-reduce(f32[5,32,16]{2,1,0:T(8,128)S(1)} %reshape.200), channel_id=1, replica_groups=mesh['stream'=8,'span'=16,'vert'=4] {'stream'}, use_global_device_ids=true, to_apply=%region_3.4 | all-reduce | flops 2560 | bytes 20480 | tf_op jit(solution)/shard_map/psum | solution.py:144
  94.0 7.5 %multiply_add_fusion = f32[5,32,16,128]{3,2,1,0:T(8,128)S(1)} fusion(f32[5,32,16,128]{3,2,1,0:T(8,128)S(1)} %copy-done.1, f32[5,32,16,128]{3,2,1,0:T(8,128)} %broadcast_dynamic-update-slice_fusion.1, f32[5,32,16]{2,1,0:T(8,128)S(1)} %broadcast_add_fusion.1, f32[128]{0:T(128)S(1)} %compare_select_fusion.1, f32[32,16,128]{2,1,0:T(8,128)} %get-tuple-element.87, ...), kind=kLoop, calls=%fused_computation.45 | loop fusion | flops 13434880 | bytes 5009844 | tf_op jit(solution)/shard_map/add | solution.py:155
  108.5 4.5 %collective-permute-start.7 = (f32[5,32,16,1]{1,2,3,0:T(8,128)S(1)}, f32[5,32,16,1]{1,2,3,0:T(8,128)S(1)}, u32[]{:S(2)}, u32[]{:S(2)}) collective-permute-start(f32[5,32,16,1]{1,2,3,0:T(8,128)S(1)} %copy.46), channel_id=1, source_target_pairs={{0,64},{64,128},{128,192},{192,256},{256,320},{320,384},{384,448},... | collective-permute-start | bytes 30728 | tf_op jit(solution)/shard_map/ppermute | solution.py:24
  116.4 2.9 %pad_maximum_fusion.36 = (f32[5,32,1,130]{3,2,1,0:T(1,128)S(1)}, f32[5,32,1,130]{3,2,1,0:T(1,128)S(1)}) fusion(f32[5,32,16,1]{3,2,1,0:T(8,128)} %copy.45, f32[5,32,16,128]{3,2,1,0:T(8,128)S(1)} %multiply_add_fusion, f32[5,32,16,1]{3,2,1,0:T(8,128)} %copy.47), kind=kLoop, calls=%fused_computation.118 | loop fusion | flops 83200 | bytes 1497600 | tf_op jit(solution)/shard_map/concatenate | solution.py:28
  119.3 2.1 collective-permute-start.8
  121.4 2.6 collective-permute-start.9
  124.2 3.8 %collective-permute-done.9 = f32[5,32,1,130]{3,2,1,0:T(1,128)S(1)} collective-permute-done((f32[5,32,1,130]{3,2,1,0:T(1,128)S(1)}, f32[5,32,1,130]{3,2,1,0:T(1,128)S(1)}, u32[]{:S(2)}, u32[]{:S(2)}) %collective-permute-start.9) | collective-permute-done | bytes 83232 | tf_op jit(solution)/shard_map/ppermute | solution.py:24
  129.5 5.0 %collective-permute-start.11 = (f32[5,1,18,130]{3,2,1,0:T(8,128)S(1)}, f32[5,1,18,130]{3,2,1,0:T(8,128)S(1)}, u32[]{:S(2)}, u32[]{:S(2)}) collective-permute-start(f32[5,1,18,130]{3,2,1,0:T(8,128)S(1)} %get-tuple-element.69), channel_id=1, source_target_pairs={{0,1},{1,2},{2,3},{4,5},{5,6},{6,7},{8,9},{9,10},{10,11},{12,13},{... | collective-permute-start | bytes 140408 | tf_op jit(solution)/shard_map/ppermute | solution.py:24
  136.9 3.1 %broadcast_multiply_fusion = (f32[5,32,16,128]{3,2,1,0:T(8,128)S(1)}, f32[5,32,16,128]{3,2,1,0:T(8,128)S(1)}) fusion(f32[5,1,18,130]{3,2,1,0:T(8,128)S(1)} %collective-permute-done.10, f32[5,32,1,130]{3,2,1,0:T(1,128)S(1)} %collective-permute-done.8, f32[5,32,16,1]{3,2,1,0:T(8,128)S(1)} %copy-done.4, f32[5,32,16,128]{3,2,1,0:T(8,128)S(1)} %multiply_add_fusion, ...), kind=kLoop, calls=%fused_computation.47 | loop fusion | flops 5242880 | bytes 4212640 | tf_op jit(solution)/shard_map/mul | solution.py:59
  140.4 5.0 %add_multiply_fusion = f32[5,32,16,128]{3,2,1,0:T(8,128)S(1)} fusion(f32[5,32,16,128]{3,2,1,0:T(8,128)S(1)} %broadcast_dynamic-update-slice_fusion, f32[5,32,16,128]{3,2,1,0:T(8,128)S(1)} %multiply_add_fusion, f32[5,32,16,128]{3,2,1,0:T(8,128)S(1)} %copy-done.1, f32[32,16,128]{2,1,0:T(8,128)S(1)} %get-tuple-element.82, ...), kind=kLoop, calls=%fused_computation.44 | loop fusion | flops 14090240 | bytes 6320564 | tf_op jit(solution)/shard_map/mul | solution.py:157
  146.5 11.8 %gather_fusion = f32[2048]{0:T(1024)S(1)} fusion(f32[65536]{0:T(1024)S(1)} %bitcast.150, s32[2048]{0:T(1024)S(1)} %broadcast_clamp_fusion), kind=kCustom, calls=%fused_computation | custom fusion | bytes 24576 | tf_op jit(solution)/shard_map/gather | solution.py:159
  158.2 16.8 %all-gather = f32[32768]{0:T(1024)S(1)} all-gather(f32[2048]{0:T(1024)S(1)} %gather_fusion), channel_id=2, replica_groups=mesh['stream'=8,'span'=16,'vert'=4] {'span'}, dimensions={0}, use_global_device_ids=true | all-gather | bytes 139264 | tf_op jit(solution)/shard_map/all_gather | solution.py:161
  175.2 10.6 %while.11 = (s32[]{:T(128)}, f32[3,64]{1,0:T(4,128)S(1)}, f32[16,3,2048]{2,0,1:T(8,128)S(1)}, s32[16,2048]{1,0:T(8,128)S(1)}, s32[]{:T(128)}, /*index=5*/s32[]{:T(128)}) while((s32[]{:T(128)}, f32[3,64]{1,0:T(4,128)S(1)}, f32[16,3,2048]{2,0,1:T(8,128)S(1)}, s32[16,2048]{1,0:T(8,128)S(1)}, s32[]{:T(128)}, /*index=5*/s32[]{:T(128)}) %tuple.46), condition=%wide.region_5.6_spmd.clone, body=%wide.region_4.5_spmd.clone.sunk | while | flops 4850051 | bytes 99927 | solution.py:104
  186.0 77.3 %psum.15 = f32[32]{0:T(128)} all-reduce(f32[32]{0:T(128)S(1)} %convolution_bitcast_fusion), channel_id=1, replica_groups=mesh['stream'=8,'span'=16,'vert'=4] {'stream','vert'}, use_global_device_ids=true, to_apply=%region_6.7 | all-reduce | flops 32 | bytes 256 | tf_op jit(solution)/shard_map/psum | solution.py:165
  (152 shorter events, 46.9 us)
Async XLA Ops:
  0.6 185.2 %copy-start = (f32[3,64,32]{1,2,0:T(8,128)S(1)}, f32[3,64,32]{1,2,0:T(8,128)}, u32[]{:S(2)}) copy-start(f32[3,64,32]{1,2,0:T(8,128)} %param.20) | copy-start | bytes 73732
  3.4 25.0 %collective-permute-start = (f32[5,32,16,1]{1,2,3,0:T(8,128)S(1)}, f32[5,32,16,1]{1,2,3,0:T(8,128)S(1)}, u32[]{:S(2)}, u32[]{:S(2)}) collective-permute-start(f32[5,32,16,1]{1,2,3,0:T(8,128)S(1)} %copy.55), channel_id=1, source_target_pairs={{64,0},{128,64},{192,128},{256,192},{320,256},{384,320},{448,384},... | collective-permute-start | bytes 30728 | tf_op jit(solution)/shard_map/ppermute | solution.py:27
  5.3 23.7 %collective-permute-start.1 = (f32[5,32,16,1]{1,2,3,0:T(8,128)S(1)}, f32[5,32,16,1]{1,2,3,0:T(8,128)S(1)}, u32[]{:S(2)}, u32[]{:S(2)}) collective-permute-start(f32[5,32,16,1]{1,2,3,0:T(8,128)S(1)} %copy.56), channel_id=1, source_target_pairs={{0,64},{64,128},{128,192},{192,256},{256,320},{320,384},{384,448},... | collective-permute-start | bytes 30728 | tf_op jit(solution)/shard_map/ppermute | solution.py:24
  10.7 14.8 %copy-start.1 = (f32[5,32,16,128]{3,2,1,0:T(8,128)S(1)}, f32[5,32,16,128]{3,2,1,0:T(8,128)}, u32[]{:S(2)}) copy-start(f32[5,32,16,128]{3,2,1,0:T(8,128)} %param.13) | copy-start | bytes 3932164
  12.2 14.2 %copy-start.13 = (s32[1,1,1,2048]{3,2,1,0:T(1,128)S(1)}, s32[1,1,1,2048]{3,2,1,0:T(1,128)}, u32[]{:S(2)}) copy-start(s32[1,1,1,2048]{3,2,1,0:T(1,128)} %param.17) | copy-start | bytes 24580
  12.2 46.5 %all-to-all-start = ((f32[64,1,2560]{2,1,0:T(1,128)}), f32[64,1,2560]{2,1,0:T(1,128)}, u32[]{:S(2)}, u32[]{:S(2)}) async-start(f32[64,1,2560]{2,1,0:T(1,128)} %all_to_all.8), calls=%async_computation | async-start | bytes 1310720 | tf_op jit(solution)/shard_map/all_to_all | solution.py:128
  29.1 22.7 %copy-start.2 = (f32[5,32,16,1]{3,2,1,0:T(8,128)}, f32[5,32,16,1]{3,2,1,0:T(8,128)S(1)}, u32[]{:S(2)}) copy-start(f32[5,32,16,1]{3,2,1,0:T(8,128)S(1)} %copy.37) | copy-start | bytes 30724
  30.7 12.4 %copy-start.3 = (f32[5,32,16,1]{3,2,1,0:T(8,128)S(1)}, f32[5,32,16,1]{3,2,1,0:T(8,128)}, u32[]{:S(2)}) copy-start(f32[5,32,16,1]{3,2,1,0:T(8,128)} %copy.39) | copy-start | bytes 30724
  33.2 8.4 %collective-permute-start.2 = (f32[5,32,1,130]{3,2,1,0:T(1,128)S(1)}, f32[5,32,1,130]{3,2,1,0:T(1,128)S(1)}, u32[]{:S(2)}, u32[]{:S(2)}) collective-permute-start(f32[5,32,1,130]{3,2,1,0:T(1,128)S(1)} %get-tuple-element.80), channel_id=1, source_target_pairs={{4,0},{8,4},{12,8},{16,12},{20,16},{24,20},{28,24},{32,28},{36,32}... | collective-permute-start | bytes 249608 | tf_op jit(solution)/shard_map/ppermute | solution.py:27
  35.2 7.9 %collective-permute-start.3 = (f32[5,32,1,130]{3,2,1,0:T(1,128)S(1)}, f32[5,32,1,130]{3,2,1,0:T(1,128)S(1)}, u32[]{:S(2)}, u32[]{:S(2)}) collective-permute-start(f32[5,32,1,130]{3,2,1,0:T(1,128)S(1)} %get-tuple-element.79), channel_id=1, source_target_pairs={{0,4},{4,8},{8,12},{12,16},{16,20},{20,24},{24,28},{28,32},{32,36}... | collective-permute-start | bytes 249608 | tf_op jit(solution)/shard_map/ppermute | solution.py:24
  43.2 7.3 %collective-permute-start.4 = (f32[5,1,18,130]{3,2,1,0:T(8,128)S(1)}, f32[5,1,18,130]{3,2,1,0:T(8,128)S(1)}, u32[]{:S(2)}, u32[]{:S(2)}) collective-permute-start(f32[5,1,18,130]{3,2,1,0:T(8,128)S(1)} %get-tuple-element.72), channel_id=1, source_target_pairs={{1,0},{2,1},{3,2},{5,4},{6,5},{7,6},{9,8},{10,9},{11,10},{13,12},{... | collective-permute-start | bytes 140408 | tf_op jit(solution)/shard_map/ppermute | solution.py:27
  44.5 7.2 %collective-permute-start.5 = (f32[5,1,18,130]{3,2,1,0:T(8,128)S(1)}, f32[5,1,18,130]{3,2,1,0:T(8,128)S(1)}, u32[]{:S(2)}, u32[]{:S(2)}) collective-permute-start(f32[5,1,18,130]{3,2,1,0:T(8,128)S(1)} %get-tuple-element.71), channel_id=1, source_target_pairs={{0,1},{1,2},{2,3},{4,5},{5,6},{6,7},{8,9},{9,10},{10,11},{12,13},{... | collective-permute-start | bytes 140408 | tf_op jit(solution)/shard_map/ppermute | solution.py:24
  61.3 32.6 %copy-start.16 = (f32[5]{0:T(128)S(1)}, f32[5]{0:T(128)}, u32[]{:S(2)}) copy-start(f32[5]{0:T(128)} %constant.116.clone) | copy-start | bytes 64
  61.4 32.6 %copy-start.15 = (f32[5]{0:T(128)S(1)}, f32[5]{0:T(128)}, u32[]{:S(2)}) copy-start(f32[5]{0:T(128)} %constant.117.clone) | copy-start | bytes 64
  103.5 9.7 %copy-start.12 = (s32[1,16,1,2048]{3,2,1,0:T(1,128)S(1)}, s32[1,16,1,2048]{3,2,1,0:T(1,128)}, u32[]{:S(2)}) copy-start(s32[1,16,1,2048]{3,2,1,0:T(1,128)} %param.19) | copy-start | bytes 393220
  105.4 7.8 %collective-permute-start.6 = (f32[5,32,16,1]{1,2,3,0:T(8,128)S(1)}, f32[5,32,16,1]{1,2,3,0:T(8,128)S(1)}, u32[]{:S(2)}, u32[]{:S(2)}) collective-permute-start(f32[5,32,16,1]{1,2,3,0:T(8,128)S(1)} %copy.44), channel_id=1, source_target_pairs={{64,0},{128,64},{192,128},{256,192},{320,256},{384,320},{448,384},... | collective-permute-start | bytes 30728 | tf_op jit(solution)/shard_map/ppermute | solution.py:27
  108.5 6.3 %collective-permute-start.7 = (f32[5,32,16,1]{1,2,3,0:T(8,128)S(1)}, f32[5,32,16,1]{1,2,3,0:T(8,128)S(1)}, u32[]{:S(2)}, u32[]{:S(2)}) collective-permute-start(f32[5,32,16,1]{1,2,3,0:T(8,128)S(1)} %copy.46), channel_id=1, source_target_pairs={{0,64},{64,128},{128,192},{192,256},{256,320},{320,384},{384,448},... | collective-permute-start | bytes 30728 | tf_op jit(solution)/shard_map/ppermute | solution.py:24
  116.4 11.6 %copy-start.5 = (f32[5,32,16,1]{3,2,1,0:T(8,128)S(1)}, f32[5,32,16,1]{3,2,1,0:T(8,128)}, u32[]{:S(2)}) copy-start(f32[5,32,16,1]{3,2,1,0:T(8,128)} %copy.47) | copy-start | bytes 30724
  119.3 8.7 %copy-start.4 = (f32[5,32,16,1]{3,2,1,0:T(8,128)S(1)}, f32[5,32,16,1]{3,2,1,0:T(8,128)}, u32[]{:S(2)}) copy-start(f32[5,32,16,1]{3,2,1,0:T(8,128)} %copy.45) | copy-start | bytes 30724
  119.3 4.9 %collective-permute-start.8 = (f32[5,32,1,130]{3,2,1,0:T(1,128)S(1)}, f32[5,32,1,130]{3,2,1,0:T(1,128)S(1)}, u32[]{:S(2)}, u32[]{:S(2)}) collective-permute-start(f32[5,32,1,130]{3,2,1,0:T(1,128)S(1)} %get-tuple-element.76), channel_id=1, source_target_pairs={{4,0},{8,4},{12,8},{16,12},{20,16},{24,20},{28,24},{32,28},{36,32}... | collective-permute-start | bytes 249608 | tf_op jit(solution)/shard_map/ppermute | solution.py:27
  121.4 6.6 %collective-permute-start.9 = (f32[5,32,1,130]{3,2,1,0:T(1,128)S(1)}, f32[5,32,1,130]{3,2,1,0:T(1,128)S(1)}, u32[]{:S(2)}, u32[]{:S(2)}) collective-permute-start(f32[5,32,1,130]{3,2,1,0:T(1,128)S(1)} %get-tuple-element.75), channel_id=1, source_target_pairs={{0,4},{4,8},{8,12},{12,16},{16,20},{20,24},{24,28},{28,32},{32,36}... | collective-permute-start | bytes 249608 | tf_op jit(solution)/shard_map/ppermute | solution.py:24
  128.2 7.4 %collective-permute-start.10 = (f32[5,1,18,130]{3,2,1,0:T(8,128)S(1)}, f32[5,1,18,130]{3,2,1,0:T(8,128)S(1)}, u32[]{:S(2)}, u32[]{:S(2)}) collective-permute-start(f32[5,1,18,130]{3,2,1,0:T(8,128)S(1)} %get-tuple-element.70), channel_id=1, source_target_pairs={{1,0},{2,1},{3,2},{5,4},{6,5},{7,6},{9,8},{10,9},{11,10},{13,12},{... | collective-permute-start | bytes 140408 | tf_op jit(solution)/shard_map/ppermute | solution.py:27
  129.5 7.4 %collective-permute-start.11 = (f32[5,1,18,130]{3,2,1,0:T(8,128)S(1)}, f32[5,1,18,130]{3,2,1,0:T(8,128)S(1)}, u32[]{:S(2)}, u32[]{:S(2)}) collective-permute-start(f32[5,1,18,130]{3,2,1,0:T(8,128)S(1)} %get-tuple-element.69), channel_id=1, source_target_pairs={{0,1},{1,2},{2,3},{4,5},{5,6},{6,7},{8,9},{9,10},{10,11},{12,13},{... | collective-permute-start | bytes 140408 | tf_op jit(solution)/shard_map/ppermute | solution.py:24
  146.4 28.6 %copy-start.10 = (f32[1,16,1,3,2048]{4,2,3,1,0:T(1,128)S(1)}, f32[1,16,1,3,2048]{4,2,3,1,0:T(1,128)}, u32[]{:S(2)}) copy-start(f32[1,16,1,3,2048]{4,2,3,1,0:T(1,128)} %param.18) | copy-start | bytes 1179652
  (6 other events, 27.6 us)
where the time goes:
time: 264 us; the launch traced here: 263 us
  blocking collectives  125 us (47%)
  starting transfers between devices  46.3 us (18%)
  other arithmetic  36.1 us (14%)
  local copies, waits for them, and re-layouts  30.7 us (12%)
  waiting for transfers between devices  12.1 us (5%)
  matrix products  11.3 us (4%)
    psum x1, blocking collectives, on_device(): modal_force = lax.psum(modal_part, ('stream', 'vert'))  77.3 us
    psum x1, blocking collectives, on_device(): lax.psum(partial_value, 'stream').reshape(5, depth_cells, span_cells)  30.8 us
    ppermute x6, starting transfers between devices, extended(): lax.ppermute(lax.slice_in_dim(block, block.shape[dim] - width, None, axis...  23.8 us
    all_gather x1, blocking collectives, on_device(): lax.all_gather(sampled.reshape(1, 1, 1, -1), 'span', axis=1, tiled=True)  16.8 us
    all_to_all x1, starting transfers between devices, on_device(): lax.all_to_all(outgoing.reshape(tile_count, CAP * 5 * spec_cols), ('span'...  13.3 us
    gather x1, local copies, waits for them, and re-layouts, on_device(): sampled = pressure[deck_cells[0, 0, 0]]  11.8 us
    dot_general x16, matrix products, add_row(): jnp.dot(row_values, member, precision=lax.Precision.HIGHEST)  9.31 us
    ppermute x6, starting transfers between devices, extended(): lax.ppermute(lax.slice_in_dim(block, 0, width, axis=dim), axis, backward)  9.23 us
  transfers between devices with their start and end apart: 13, of which 7 were waited for; matrix products, arithmetic and copies ran while one was open for 8% of the time, Pallas kernels for 0%

commit v1 on v0

--- a/solution.py
+++ b/solution.py
@@ -162,7 +162,7 @@
     traction = rows_all[0, :, 0][:, None, :] * deck_geom[0, :, 0]
     forces = strip_forces(traction, strip_ids[0, :, 0], strip_count)
     modal_part = jnp.einsum("cj,cjm->m", forces, mode_shapes, precision=lax.Precision.HIGHEST)
-    modal_force = lax.psum(modal_part, ("stream", "vert"))
+    modal_force = lax.psum(lax.psum(modal_part, "vert"), "stream")
     return (new_fields, modal_force)
 
 

time: 264 us -> 217 us (0.82)
  the two profiles are of different devices: /device:TPU:64 before, /device:TPU:24 now
where the time goes in v1:
time: 217 us
  blocking collectives  82.1 us (38%)
  starting transfers between devices  49.6 us (23%)
  other arithmetic  36.1 us (17%)
  local copies, waits for them, and re-layouts  30.7 us (14%)
  matrix products  11.3 us (5%)
  waiting for transfers between devices  4.84 us (2%)
    psum x2, blocking collectives, on_device(): modal_force = lax.psum(lax.psum(modal_part, 'vert'), 'stream')  28.5 us
    psum x1, blocking collectives, on_device(): lax.psum(partial_value, 'stream').reshape(5, depth_cells, span_cells)  28.1 us
    all_gather x1, blocking collectives, on_device(): lax.all_gather(sampled.reshape(1, 1, 1, -1), 'span', axis=1, tiled=True)  25.6 us
    ppermute x6, starting transfers between devices, extended(): lax.ppermute(lax.slice_in_dim(block, block.shape[dim] - width, None, axis...  24.2 us
    all_to_all x1, starting transfers between devices, on_device(): lax.all_to_all(outgoing.reshape(tile_count, CAP * 5 * spec_cols), ('span'...  14.1 us
    gather x1, local copies, waits for them, and re-layouts, on_device(): sampled = pressure[deck_cells[0, 0, 0]]  11.8 us
    ppermute x6, starting transfers between devices, extended(): lax.ppermute(lax.slice_in_dim(block, 0, width, axis=dim), axis, backward)  11.3 us
    dot_general x16, matrix products, add_row(): jnp.dot(row_values, member, precision=lax.Precision.HIGHEST)  9.31 us
  transfers between devices with their start and end apart: 13, of which 5 were waited for; matrix products, arithmetic and copies ran while one was open for 10% of the time, Pallas kernels for 0%

profile of v1, /device:TPU:24, one launch (start us, length us, event | category | flops | bytes accessed | tf_op | source)
XLA Modules:
  0.0 216.7 jit_solution(39878756111789206)
XLA Ops:
  0.6 2.2 fusion.52
  3.4 2.4 %collective-permute-start = (f32[5,32,16,1]{1,2,3,0:T(8,128)S(1)}, f32[5,32,16,1]{1,2,3,0:T(8,128)S(1)}, u32[]{:S(2)}, u32[]{:S(2)}) collective-permute-start(f32[5,32,16,1]{1,2,3,0:T(8,128)S(1)} %copy.55), channel_id=1, source_target_pairs={{64,0},{128,64},{192,128},{256,192},{320,256},{384,320},{448,384},... | collective-permute-start | bytes 30728 | tf_op jit(solution)/shard_map/ppermute | solution.py:27
  6.4 4.7 %collective-permute-start.1 = (f32[5,32,16,1]{1,2,3,0:T(8,128)S(1)}, f32[5,32,16,1]{1,2,3,0:T(8,128)S(1)}, u32[]{:S(2)}, u32[]{:S(2)}) collective-permute-start(f32[5,32,16,1]{1,2,3,0:T(8,128)S(1)} %copy.56), channel_id=1, source_target_pairs={{0,64},{64,128},{128,192},{192,256},{256,320},{320,384},{384,448},... | collective-permute-start | bytes 30728 | tf_op jit(solution)/shard_map/ppermute | solution.py:24
  13.5 14.1 %all-to-all-start = ((f32[64,1,2560]{2,1,0:T(1,128)}), f32[64,1,2560]{2,1,0:T(1,128)}, u32[]{:S(2)}, u32[]{:S(2)}) async-start(f32[64,1,2560]{2,1,0:T(1,128)} %all_to_all.8), calls=%async_computation | async-start | bytes 1310720 | tf_op jit(solution)/shard_map/all_to_all | solution.py:128
  32.8 2.5 %pad_maximum_fusion.39 = (f32[5,32,1,130]{3,2,1,0:T(1,128)S(1)}, f32[5,32,1,130]{3,2,1,0:T(1,128)S(1)}) fusion(f32[5,32,16,1]{3,2,1,0:T(8,128)S(1)} %copy.37, f32[5,32,16,128]{3,2,1,0:T(8,128)S(1)} %copy-done.1, f32[5,32,16,1]{3,2,1,0:T(8,128)} %copy.39), kind=kLoop, calls=%fused_computation.121 | loop fusion | flops 83200 | bytes 1497600 | tf_op jit(solution)/shard_map/concatenate | solution.py:28
  36.6 3.0 %collective-permute-start.3 = (f32[5,32,1,130]{3,2,1,0:T(1,128)S(1)}, f32[5,32,1,130]{3,2,1,0:T(1,128)S(1)}, u32[]{:S(2)}, u32[]{:S(2)}) collective-permute-start(f32[5,32,1,130]{3,2,1,0:T(1,128)S(1)} %get-tuple-element.79), channel_id=1, source_target_pairs={{0,4},{4,8},{8,12},{12,16},{16,20},{20,24},{24,28},{28,32},{32,36}... | collective-permute-start | bytes 249608 | tf_op jit(solution)/shard_map/ppermute | solution.py:24
  42.1 4.7 %collective-permute-start.5 = (f32[5,1,18,130]{3,2,1,0:T(8,128)S(1)}, f32[5,1,18,130]{3,2,1,0:T(8,128)S(1)}, u32[]{:S(2)}, u32[]{:S(2)}) collective-permute-start(f32[5,1,18,130]{3,2,1,0:T(8,128)S(1)} %get-tuple-element.71), channel_id=1, source_target_pairs={{0,1},{1,2},{2,3},{4,5},{5,6},{6,7},{8,9},{9,10},{10,11},{12,13},{... | collective-permute-start | bytes 140408 | tf_op jit(solution)/shard_map/ppermute | solution.py:24
  49.1 3.2 %broadcast_multiply_fusion.3 = (f32[5,32,16,128]{3,2,1,0:T(8,128)S(1)}, f32[5,32,16,128]{3,2,1,0:T(8,128)S(1)}) fusion(f32[5,1,18,130]{3,2,1,0:T(8,128)S(1)} %collective-permute-done.4, f32[5,32,1,130]{3,2,1,0:T(1,128)S(1)} %collective-permute-done.2, f32[5,32,16,1]{3,2,1,0:T(8,128)S(1)} %copy.37, f32[5,32,16,128]{3,2,1,0:T(8,128)S(1)} %copy-done.1, ...), kind=kLoop, calls=%fused_computation.50 | loop fusion | flops 5242880 | bytes 4212640 | tf_op jit(solution)/shard_map/mul | solution.py:59
  56.1 2.6 %reduce = f32[64,2560]{1,0:T(8,128)S(1)} reduce(f32[64,1,2560]{2,1,0:T(1,128)} %all-to-all-done, f32[]{:T(128)} %constant.123), dimensions={1}, to_apply=%all_to_all.7.reduce_sub_computation | reduce | bytes 1310724 | tf_op jit(solution)/shard_map/all_to_all | solution.py:128
  60.5 28.1 %psum.21 = f32[5,32,16]{2,1,0:T(8,128)S(1)} all-reduce(f32[5,32,16]{2,1,0:T(8,128)S(1)} %reshape.200), channel_id=1, replica_groups=mesh['stream'=8,'span'=16,'vert'=4] {'stream'}, use_global_device_ids=true, to_apply=%region_3.4 | all-reduce | flops 2560 | bytes 20480 | tf_op jit(solution)/shard_map/psum | solution.py:144
  88.6 7.5 %multiply_add_fusion = f32[5,32,16,128]{3,2,1,0:T(8,128)S(1)} fusion(f32[5,32,16,128]{3,2,1,0:T(8,128)S(1)} %copy-done.1, f32[5,32,16,128]{3,2,1,0:T(8,128)} %broadcast_dynamic-update-slice_fusion.1, f32[5,32,16]{2,1,0:T(8,128)S(1)} %broadcast_add_fusion.1, f32[128]{0:T(128)S(1)} %compare_select_fusion.1, f32[32,16,128]{2,1,0:T(8,128)} %get-tuple-element.87, ...), kind=kLoop, calls=%fused_computation.45 | loop fusion | flops 13434880 | bytes 5009844 | tf_op jit(solution)/shard_map/add | solution.py:155
  96.1 1.9 fusion.51
  100.0 3.6 %collective-permute-start.6 = (f32[5,32,16,1]{1,2,3,0:T(8,128)S(1)}, f32[5,32,16,1]{1,2,3,0:T(8,128)S(1)}, u32[]{:S(2)}, u32[]{:S(2)}) collective-permute-start(f32[5,32,16,1]{1,2,3,0:T(8,128)S(1)} %copy.44), channel_id=1, source_target_pairs={{64,0},{128,64},{192,128},{256,192},{320,256},{384,320},{448,384},... | collective-permute-start | bytes 30728 | tf_op jit(solution)/shard_map/ppermute | solution.py:27
  105.5 3.4 %collective-permute-start.7 = (f32[5,32,16,1]{1,2,3,0:T(8,128)S(1)}, f32[5,32,16,1]{1,2,3,0:T(8,128)S(1)}, u32[]{:S(2)}, u32[]{:S(2)}) collective-permute-start(f32[5,32,16,1]{1,2,3,0:T(8,128)S(1)} %copy.46), channel_id=1, source_target_pairs={{0,64},{64,128},{128,192},{192,256},{256,320},{320,384},{384,448},... | collective-permute-start | bytes 30728 | tf_op jit(solution)/shard_map/ppermute | solution.py:24
  113.0 2.9 %pad_maximum_fusion.36 = (f32[5,32,1,130]{3,2,1,0:T(1,128)S(1)}, f32[5,32,1,130]{3,2,1,0:T(1,128)S(1)}) fusion(f32[5,32,16,1]{3,2,1,0:T(8,128)} %copy.45, f32[5,32,16,128]{3,2,1,0:T(8,128)S(1)} %multiply_add_fusion, f32[5,32,16,1]{3,2,1,0:T(8,128)} %copy.47), kind=kLoop, calls=%fused_computation.118 | loop fusion | flops 83200 | bytes 1497600 | tf_op jit(solution)/shard_map/concatenate | solution.py:28
  117.3 3.3 %collective-permute-start.9 = (f32[5,32,1,130]{3,2,1,0:T(1,128)S(1)}, f32[5,32,1,130]{3,2,1,0:T(1,128)S(1)}, u32[]{:S(2)}, u32[]{:S(2)}) collective-permute-start(f32[5,32,1,130]{3,2,1,0:T(1,128)S(1)} %get-tuple-element.75), channel_id=1, source_target_pairs={{0,4},{4,8},{8,12},{12,16},{16,20},{20,24},{24,28},{28,32},{32,36}... | collective-permute-start | bytes 249608 | tf_op jit(solution)/shard_map/ppermute | solution.py:24
  122.8 5.1 %collective-permute-start.11 = (f32[5,1,18,130]{3,2,1,0:T(8,128)S(1)}, f32[5,1,18,130]{3,2,1,0:T(8,128)S(1)}, u32[]{:S(2)}, u32[]{:S(2)}) collective-permute-start(f32[5,1,18,130]{3,2,1,0:T(8,128)S(1)} %get-tuple-element.69), channel_id=1, source_target_pairs={{0,1},{1,2},{2,3},{4,5},{5,6},{6,7},{8,9},{9,10},{10,11},{12,13},{... | collective-permute-start | bytes 140408 | tf_op jit(solution)/shard_map/ppermute | solution.py:24
  130.3 3.1 %broadcast_multiply_fusion = (f32[5,32,16,128]{3,2,1,0:T(8,128)S(1)}, f32[5,32,16,128]{3,2,1,0:T(8,128)S(1)}) fusion(f32[5,1,18,130]{3,2,1,0:T(8,128)S(1)} %collective-permute-done.10, f32[5,32,1,130]{3,2,1,0:T(1,128)S(1)} %collective-permute-done.8, f32[5,32,16,1]{3,2,1,0:T(8,128)S(1)} %copy-done.4, f32[5,32,16,128]{3,2,1,0:T(8,128)S(1)} %multiply_add_fusion, ...), kind=kLoop, calls=%fused_computation.47 | loop fusion | flops 5242880 | bytes 4212640 | tf_op jit(solution)/shard_map/mul | solution.py:59
  133.8 5.0 %add_multiply_fusion = f32[5,32,16,128]{3,2,1,0:T(8,128)S(1)} fusion(f32[5,32,16,128]{3,2,1,0:T(8,128)S(1)} %broadcast_dynamic-update-slice_fusion, f32[5,32,16,128]{3,2,1,0:T(8,128)S(1)} %multiply_add_fusion, f32[5,32,16,128]{3,2,1,0:T(8,128)S(1)} %copy-done.1, f32[32,16,128]{2,1,0:T(8,128)S(1)} %get-tuple-element.82, ...), kind=kLoop, calls=%fused_computation.44 | loop fusion | flops 14090240 | bytes 6320564 | tf_op jit(solution)/shard_map/mul | solution.py:157
  139.9 11.8 %gather_fusion = f32[2048]{0:T(1024)S(1)} fusion(f32[65536]{0:T(1024)S(1)} %bitcast.150, s32[2048]{0:T(1024)S(1)} %broadcast_clamp_fusion), kind=kCustom, calls=%fused_computation | custom fusion | bytes 24576 | tf_op jit(solution)/shard_map/gather | solution.py:159
  151.7 25.6 %all-gather = f32[32768]{0:T(1024)S(1)} all-gather(f32[2048]{0:T(1024)S(1)} %gather_fusion), channel_id=2, replica_groups=mesh['stream'=8,'span'=16,'vert'=4] {'span'}, dimensions={0}, use_global_device_ids=true | all-gather | bytes 139264 | tf_op jit(solution)/shard_map/all_gather | solution.py:161
  177.4 10.6 %while.11 = (s32[]{:T(128)}, f32[3,64]{1,0:T(4,128)S(1)}, f32[16,3,2048]{2,0,1:T(8,128)S(1)}, s32[16,2048]{1,0:T(8,128)S(1)}, s32[]{:T(128)}, /*index=5*/s32[]{:T(128)}) while((s32[]{:T(128)}, f32[3,64]{1,0:T(4,128)S(1)}, f32[16,3,2048]{2,0,1:T(8,128)S(1)}, s32[16,2048]{1,0:T(8,128)S(1)}, s32[]{:T(128)}, /*index=5*/s32[]{:T(128)}) %tuple.46), condition=%wide.region_5.6_spmd.clone, body=%wide.region_4.5_spmd.clone.sunk | while | flops 4850051 | bytes 99927 | solution.py:104
  188.2 12.4 %psum.22 = f32[32]{0:T(128)S(1)} all-reduce(f32[32]{0:T(128)S(1)} %convolution_bitcast_fusion), channel_id=1, replica_groups=mesh['stream'=8,'span'=16,'vert'=4] {'vert'}, use_global_device_ids=true, to_apply=%region_6.7 | all-reduce | flops 32 | bytes 256 | tf_op jit(solution)/shard_map/psum | solution.py:165
  200.6 16.1 %psum.23 = f32[32]{0:T(128)} all-reduce(f32[32]{0:T(128)S(1)} %psum.22), channel_id=1, replica_groups=mesh['stream'=8,'span'=16,'vert'=4] {'stream'}, use_global_device_ids=true, to_apply=%region_7.8 | all-reduce | flops 32 | bytes 256 | tf_op jit(solution)/shard_map/psum | solution.py:165
  (153 shorter events, 45.7 us)
Async XLA Ops:
  0.6 187.4 %copy-start = (f32[3,64,32]{1,2,0:T(8,128)S(1)}, f32[3,64,32]{1,2,0:T(8,128)}, u32[]{:S(2)}) copy-start(f32[3,64,32]{1,2,0:T(8,128)} %param.20) | copy-start | bytes 73732
  2.8 8.3 %copy-start.14 = (s32[64,1]{0,1:T(1,128)S(1)}, s32[64,1]{0,1:T(1,128)}, u32[]{:S(2)}) copy-start(s32[64,1]{0,1:T(1,128)} %param.16) | copy-start | bytes 772
  2.8 8.7 %copy-start.11 = (f32[64,5,256]{2,0,1:T(8,128)S(1)}, f32[64,5,256]{2,0,1:T(8,128)}, u32[]{:S(2)}) copy-start(f32[64,5,256]{2,0,1:T(8,128)} %param.15) | copy-start | bytes 983044
  3.4 27.1 %collective-permute-start = (f32[5,32,16,1]{1,2,3,0:T(8,128)S(1)}, f32[5,32,16,1]{1,2,3,0:T(8,128)S(1)}, u32[]{:S(2)}, u32[]{:S(2)}) collective-permute-start(f32[5,32,16,1]{1,2,3,0:T(8,128)S(1)} %copy.55), channel_id=1, source_target_pairs={{64,0},{128,64},{192,128},{256,192},{320,256},{384,320},{448,384},... | collective-permute-start | bytes 30728 | tf_op jit(solution)/shard_map/ppermute | solution.py:27
  6.4 24.8 %collective-permute-start.1 = (f32[5,32,16,1]{1,2,3,0:T(8,128)S(1)}, f32[5,32,16,1]{1,2,3,0:T(8,128)S(1)}, u32[]{:S(2)}, u32[]{:S(2)}) collective-permute-start(f32[5,32,16,1]{1,2,3,0:T(8,128)S(1)} %copy.56), channel_id=1, source_target_pairs={{0,64},{64,128},{128,192},{192,256},{256,320},{320,384},{384,448},... | collective-permute-start | bytes 30728 | tf_op jit(solution)/shard_map/ppermute | solution.py:24
  11.9 15.7 %copy-start.1 = (f32[5,32,16,128]{3,2,1,0:T(8,128)S(1)}, f32[5,32,16,128]{3,2,1,0:T(8,128)}, u32[]{:S(2)}) copy-start(f32[5,32,16,128]{3,2,1,0:T(8,128)} %param.13) | copy-start | bytes 3932164
  13.5 15.1 %copy-start.13 = (s32[1,1,1,2048]{3,2,1,0:T(1,128)S(1)}, s32[1,1,1,2048]{3,2,1,0:T(1,128)}, u32[]{:S(2)}) copy-start(s32[1,1,1,2048]{3,2,1,0:T(1,128)} %param.17) | copy-start | bytes 24580
  13.5 42.6 %all-to-all-start = ((f32[64,1,2560]{2,1,0:T(1,128)}), f32[64,1,2560]{2,1,0:T(1,128)}, u32[]{:S(2)}, u32[]{:S(2)}) async-start(f32[64,1,2560]{2,1,0:T(1,128)} %all_to_all.8), calls=%async_computation | async-start | bytes 1310720 | tf_op jit(solution)/shard_map/all_to_all | solution.py:128
  31.2 17.9 %copy-start.2 = (f32[5,32,16,1]{3,2,1,0:T(8,128)}, f32[5,32,16,1]{3,2,1,0:T(8,128)S(1)}, u32[]{:S(2)}) copy-start(f32[5,32,16,1]{3,2,1,0:T(8,128)S(1)} %copy.37) | copy-start | bytes 30724
  35.3 4.4 %collective-permute-start.2 = (f32[5,32,1,130]{3,2,1,0:T(1,128)S(1)}, f32[5,32,1,130]{3,2,1,0:T(1,128)S(1)}, u32[]{:S(2)}, u32[]{:S(2)}) collective-permute-start(f32[5,32,1,130]{3,2,1,0:T(1,128)S(1)} %get-tuple-element.80), channel_id=1, source_target_pairs={{4,0},{8,4},{12,8},{16,12},{20,16},{24,20},{28,24},{32,28},{36,32}... | collective-permute-start | bytes 249608 | tf_op jit(solution)/shard_map/ppermute | solution.py:27
  36.6 4.0 %collective-permute-start.3 = (f32[5,32,1,130]{3,2,1,0:T(1,128)S(1)}, f32[5,32,1,130]{3,2,1,0:T(1,128)S(1)}, u32[]{:S(2)}, u32[]{:S(2)}) collective-permute-start(f32[5,32,1,130]{3,2,1,0:T(1,128)S(1)} %get-tuple-element.79), channel_id=1, source_target_pairs={{0,4},{4,8},{8,12},{12,16},{16,20},{20,24},{24,28},{28,32},{32,36}... | collective-permute-start | bytes 249608 | tf_op jit(solution)/shard_map/ppermute | solution.py:24
  40.8 7.2 %collective-permute-start.4 = (f32[5,1,18,130]{3,2,1,0:T(8,128)S(1)}, f32[5,1,18,130]{3,2,1,0:T(8,128)S(1)}, u32[]{:S(2)}, u32[]{:S(2)}) collective-permute-start(f32[5,1,18,130]{3,2,1,0:T(8,128)S(1)} %get-tuple-element.72), channel_id=1, source_target_pairs={{1,0},{2,1},{3,2},{5,4},{6,5},{7,6},{9,8},{10,9},{11,10},{13,12},{... | collective-permute-start | bytes 140408 | tf_op jit(solution)/shard_map/ppermute | solution.py:27
  42.1 7.0 %collective-permute-start.5 = (f32[5,1,18,130]{3,2,1,0:T(8,128)S(1)}, f32[5,1,18,130]{3,2,1,0:T(8,128)S(1)}, u32[]{:S(2)}, u32[]{:S(2)}) collective-permute-start(f32[5,1,18,130]{3,2,1,0:T(8,128)S(1)} %get-tuple-element.71), channel_id=1, source_target_pairs={{0,1},{1,2},{2,3},{4,5},{5,6},{6,7},{8,9},{9,10},{10,11},{12,13},{... | collective-permute-start | bytes 140408 | tf_op jit(solution)/shard_map/ppermute | solution.py:24
  58.7 29.8 %copy-start.16 = (f32[5]{0:T(128)S(1)}, f32[5]{0:T(128)}, u32[]{:S(2)}) copy-start(f32[5]{0:T(128)} %constant.116.clone) | copy-start | bytes 64
  58.7 29.9 %copy-start.15 = (f32[5]{0:T(128)S(1)}, f32[5]{0:T(128)}, u32[]{:S(2)}) copy-start(f32[5]{0:T(128)} %constant.117.clone) | copy-start | bytes 64
  98.1 10.9 %copy-start.12 = (s32[1,16,1,2048]{3,2,1,0:T(1,128)S(1)}, s32[1,16,1,2048]{3,2,1,0:T(1,128)}, u32[]{:S(2)}) copy-start(s32[1,16,1,2048]{3,2,1,0:T(1,128)} %param.19) | copy-start | bytes 393220
  100.0 9.0 %collective-permute-start.6 = (f32[5,32,16,1]{1,2,3,0:T(8,128)S(1)}, f32[5,32,16,1]{1,2,3,0:T(8,128)S(1)}, u32[]{:S(2)}, u32[]{:S(2)}) collective-permute-start(f32[5,32,16,1]{1,2,3,0:T(8,128)S(1)} %copy.44), channel_id=1, source_target_pairs={{64,0},{128,64},{192,128},{256,192},{320,256},{384,320},{448,384},... | collective-permute-start | bytes 30728 | tf_op jit(solution)/shard_map/ppermute | solution.py:27
  105.5 5.9 %collective-permute-start.7 = (f32[5,32,16,1]{1,2,3,0:T(8,128)S(1)}, f32[5,32,16,1]{1,2,3,0:T(8,128)S(1)}, u32[]{:S(2)}, u32[]{:S(2)}) collective-permute-start(f32[5,32,16,1]{1,2,3,0:T(8,128)S(1)} %copy.46), channel_id=1, source_target_pairs={{0,64},{64,128},{128,192},{192,256},{256,320},{320,384},{384,448},... | collective-permute-start | bytes 30728 | tf_op jit(solution)/shard_map/ppermute | solution.py:24
  113.0 8.4 %copy-start.5 = (f32[5,32,16,1]{3,2,1,0:T(8,128)S(1)}, f32[5,32,16,1]{3,2,1,0:T(8,128)}, u32[]{:S(2)}) copy-start(f32[5,32,16,1]{3,2,1,0:T(8,128)} %copy.47) | copy-start | bytes 30724
  115.9 4.8 %collective-permute-start.8 = (f32[5,32,1,130]{3,2,1,0:T(1,128)S(1)}, f32[5,32,1,130]{3,2,1,0:T(1,128)S(1)}, u32[]{:S(2)}, u32[]{:S(2)}) collective-permute-start(f32[5,32,1,130]{3,2,1,0:T(1,128)S(1)} %get-tuple-element.76), channel_id=1, source_target_pairs={{4,0},{8,4},{12,8},{16,12},{20,16},{24,20},{28,24},{32,28},{36,32}... | collective-permute-start | bytes 249608 | tf_op jit(solution)/shard_map/ppermute | solution.py:27
  117.3 4.0 %collective-permute-start.9 = (f32[5,32,1,130]{3,2,1,0:T(1,128)S(1)}, f32[5,32,1,130]{3,2,1,0:T(1,128)S(1)}, u32[]{:S(2)}, u32[]{:S(2)}) collective-permute-start(f32[5,32,1,130]{3,2,1,0:T(1,128)S(1)} %get-tuple-element.75), channel_id=1, source_target_pairs={{0,4},{4,8},{8,12},{12,16},{16,20},{20,24},{24,28},{28,32},{32,36}... | collective-permute-start | bytes 249608 | tf_op jit(solution)/shard_map/ppermute | solution.py:24
  121.5 7.5 %collective-permute-start.10 = (f32[5,1,18,130]{3,2,1,0:T(8,128)S(1)}, f32[5,1,18,130]{3,2,1,0:T(8,128)S(1)}, u32[]{:S(2)}, u32[]{:S(2)}) collective-permute-start(f32[5,1,18,130]{3,2,1,0:T(8,128)S(1)} %get-tuple-element.70), channel_id=1, source_target_pairs={{1,0},{2,1},{3,2},{5,4},{6,5},{7,6},{9,8},{10,9},{11,10},{13,12},{... | collective-permute-start | bytes 140408 | tf_op jit(solution)/shard_map/ppermute | solution.py:27
  122.8 7.5 %collective-permute-start.11 = (f32[5,1,18,130]{3,2,1,0:T(8,128)S(1)}, f32[5,1,18,130]{3,2,1,0:T(8,128)S(1)}, u32[]{:S(2)}, u32[]{:S(2)}) collective-permute-start(f32[5,1,18,130]{3,2,1,0:T(8,128)S(1)} %get-tuple-element.69), channel_id=1, source_target_pairs={{0,1},{1,2},{2,3},{4,5},{5,6},{6,7},{8,9},{9,10},{10,11},{12,13},{... | collective-permute-start | bytes 140408 | tf_op jit(solution)/shard_map/ppermute | solution.py:24
  139.9 37.4 %copy-start.10 = (f32[1,16,1,3,2048]{4,2,3,1,0:T(1,128)S(1)}, f32[1,16,1,3,2048]{4,2,3,1,0:T(1,128)}, u32[]{:S(2)}) copy-start(f32[1,16,1,3,2048]{4,2,3,1,0:T(1,128)} %param.18) | copy-start | bytes 1179652
  (6 other events, 26.2 us)
